TPU v7x, 32 devices: a whole 2x2x4 slice. The times are simulated.
32 devices in a mesh: groups: 2 (over y), sample: 2 (over core), space: 8 (over z, x).
Axes of the slice: x: 2, y: 2, z: 4, core: 2. Of those that a mesh axis runs over, the one named last changes fastest.
Arguments:
- features: bfloat16 [4, 16, 16, 16, 128], P(('groups', 'sample'), 'space'), parts along dimension 0, may hold values from -6 to 6
- w_fine: bfloat16 [27, 128, 128], replicated, may hold values from -0.109375 to 0.109375
- w_down: bfloat16 [8, 128, 256], replicated, may hold values from -0.1875 to 0.1875
- mixing: bfloat16 [8, 8], replicated, may hold values from -2 to 2
- cotangent: bfloat16 [4, 8, 16384], P(('groups', 'sample'), None, 'space'), parts along dimension 0, may hold values from -6 to 6
Outputs:
- bottleneck: bfloat16 [4, 8, 16384], P(('groups', 'sample'), None, 'space'), parts along dimension 0
- feature_grad: bfloat16 [4, 16, 16, 16, 128], P(('groups', 'sample'), 'space'), parts along dimension 0
- fine_grad: float32 [884736], P(('groups', 'space')), parts along dimension 0
- down_grad: float32 [524288], P(('groups', 'space')), parts along dimension 0
- mixing_grad: float32 [16, 8], P(('groups', 'space')), parts along dimension 0
There are 2 independent parts, one for each index of `groups`. A program takes and returns all parts, laid end to end along the dimension named above; an argument that names none is the same for every part. Nothing has to cross between parts.
All inputs are finite; a program needn't handle non-finite values.
Results may differ from a plain program's by a relative error of at most 0.0065.
Values may be sent and summed in bfloat16 or wider, within the bound.
A program may use at most 64 MiB of HBM per device.

v0:
```python
import jax
import jax.numpy as jnp
from jax import lax
from jax.sharding import PartitionSpec as P


def with_halo(array, sides, width):
    for axis, dim in sides:
        devices, length = (lax.axis_size(axis), array.shape[dim])
        up = [(i, (i + 1) % devices) for i in range(devices - 1)]
        down = [(j, i) for i, j in up]
        last = lax.slice_in_dim(array, length - width, length, axis=dim)
        initial = lax.slice_in_dim(array, 0, width, axis=dim)
        before = lax.ppermute(last, axis, up)
        after = lax.ppermute(initial, axis, down)
        array = jnp.concatenate([before, array, after], axis=dim)
    return array


def forward_conv(padded, weight, count):
    extent_x = padded.shape[2] - 2
    extent_z = padded.shape[3] - 2
    channels = padded.shape[4]
    total = None
    for shift_y in range(3):
        for shift_x in range(3):
            pieces = [
                padded[
                    :,
                    shift_y : shift_y + count,
                    shift_x : shift_x + extent_x,
                    shift_z : shift_z + extent_z,
                    :,
                ]
                for shift_z in range(3)
            ]
            stacked = jnp.concatenate(pieces, axis=-1).reshape(-1, 3 * channels)
            first = shift_y * 9 + shift_x * 3
            kernel = weight[first : first + 3].reshape(3 * channels, weight.shape[2])
            term = jnp.dot(stacked, kernel, preferred_element_type=jnp.float32)
            total = term if total is None else total + term
    return total.reshape(padded.shape[0], count, extent_x, extent_z, weight.shape[2])


def transposed_conv(padded, weight, count):
    extent_x = padded.shape[2] - 2
    extent_z = padded.shape[3] - 2
    channels = padded.shape[4]
    total = None
    for shift_y in range(3):
        for shift_x in range(3):
            pieces = [
                padded[
                    :,
                    2 - shift_y : 2 - shift_y + count,
                    2 - shift_x : 2 - shift_x + extent_x,
                    2 - shift_z : 2 - shift_z + extent_z,
                    :,
                ]
                for shift_z in range(3)
            ]
            stacked = jnp.concatenate(pieces, axis=-1).reshape(-1, 3 * channels)
            first = shift_y * 9 + shift_x * 3
            kernel = jnp.swapaxes(weight[first : first + 3], 1, 2).reshape(
                3 * channels, weight.shape[1]
            )
            term = jnp.dot(stacked, kernel, preferred_element_type=jnp.float32)
            total = term if total is None else total + term
    return total.reshape(padded.shape[0], count, extent_x, extent_z, weight.shape[1])


def weight_terms(padded, grad, count):
    extent_x = padded.shape[2] - 2
    extent_z = padded.shape[3] - 2
    channels = padded.shape[4]
    flat_grad = grad.reshape(-1, grad.shape[4])
    blocks = []
    for shift_y in range(3):
        for shift_x in range(3):
            pieces = [
                padded[
                    :,
                    shift_y : shift_y + count,
                    shift_x : shift_x + extent_x,
                    shift_z : shift_z + extent_z,
                    :,
                ]
                for shift_z in range(3)
            ]
            stacked = jnp.concatenate(pieces, axis=-1).reshape(-1, 3 * channels)
            blocks.append(
                lax.dot_general(
                    stacked, flat_grad, (((0,), (0,)), ((), ())), preferred_element_type=jnp.float32
                )
            )
    return jnp.concatenate(blocks, axis=0).reshape(-1)


def fold_taps(hidden):
    batch, rows_here, extent_x, extent_z, channels = hidden.shape
    shaped = hidden.reshape(batch, rows_here // 2, 2, extent_x // 2, 2, extent_z // 2, 2, channels)
    return shaped.transpose(0, 1, 3, 5, 2, 4, 6, 7).reshape(-1, 8 * channels)


def unfold_taps(values, batch, rows_here, extent_x, extent_z, channels):
    shaped = values.reshape(batch, rows_here // 2, extent_x // 2, extent_z // 2, 2, 2, 2, channels)
    return shaped.transpose(0, 1, 4, 2, 5, 3, 6, 7).reshape(
        batch, rows_here, extent_x, extent_z, channels
    )


def silu_slope(value):
    sigma = jax.nn.sigmoid(value)
    return sigma * (1.0 + value * (1.0 - sigma))


def local(features, w_fine, w_down, mixing, cotangent):
    batch, rows_here, extent_x, extent_z, channels = features.shape
    coarse_ch = w_down.shape[2]
    rimmed = with_halo(features, (("space", 1),), 1)
    xpadded = jnp.pad(rimmed, ((0, 0), (0, 0), (1, 1), (1, 1), (0, 0)))
    act = forward_conv(xpadded, w_fine, rows_here)
    hidden = (features.astype(jnp.float32) + jax.nn.silu(act)).astype(jnp.bfloat16)
    folded = fold_taps(hidden)
    down_matrix = w_down.reshape(8 * channels, coarse_ch)
    coarse = jnp.dot(folded, down_matrix, preferred_element_type=jnp.float32).astype(jnp.bfloat16)
    coarse = coarse.reshape(batch, rows_here // 2, -1)
    columns = lax.all_to_all(coarse, "space", split_axis=2, concat_axis=1, tiled=True)
    mixed = jnp.stack([jnp.dot(mixing, columns[0], preferred_element_type=jnp.float32)])
    bottleneck = (columns.astype(jnp.float32) + jax.nn.silu(mixed)).astype(jnp.bfloat16)
    cot = cotangent.astype(jnp.float32)
    mixed_grad = (cot * silu_slope(mixed)).astype(jnp.bfloat16)
    term = lax.dot_general(
        mixed_grad[0], columns[0], (((1,), (1,)), ((), ())), preferred_element_type=jnp.float32
    )
    spread_list = [
        lax.dot_general(
            mixing, mixed_grad[0], (((0,), (0,)), ((), ())), preferred_element_type=jnp.float32
        )
    ]
    column_grad = (cot + jnp.stack(spread_list)).astype(jnp.bfloat16)
    coarse_grad = lax.all_to_all(column_grad, "space", split_axis=1, concat_axis=2, tiled=True)
    flat_coarse = coarse_grad.reshape(-1, coarse_ch)
    down_terms = lax.dot_general(
        folded, flat_coarse, (((0,), (0,)), ((), ())), preferred_element_type=jnp.float32
    ).reshape(-1)
    hidden_grad = unfold_taps(
        jnp.dot(flat_coarse, down_matrix.T, preferred_element_type=jnp.float32),
        batch,
        rows_here,
        extent_x,
        extent_z,
        channels,
    )
    act_grad = (hidden_grad * silu_slope(act)).astype(jnp.bfloat16)
    grad_rim = with_halo(act_grad, (("space", 1),), 1)
    gpadded = jnp.pad(grad_rim, ((0, 0), (0, 0), (1, 1), (1, 1), (0, 0)))
    spread = transposed_conv(gpadded, w_fine, rows_here)
    feature_grad = (hidden_grad + spread).astype(jnp.bfloat16)
    fine_terms = weight_terms(xpadded, act_grad, rows_here)
    scale = float(
        batch * lax.axis_size("sample") * rows_here * lax.axis_size("space") * extent_x * extent_z
    ) ** (-0.5)
    shares = (
        lax.psum_scatter(fine_terms, "space", scatter_dimension=0, tiled=True),
        lax.psum_scatter(down_terms, "space", scatter_dimension=0, tiled=True),
        lax.psum_scatter(term, "space", scatter_dimension=0, tiled=True),
    )
    totals = lax.psum((shares[0], shares[1], shares[2]), "sample")
    return (bottleneck, feature_grad, totals[0] * scale, totals[1] * scale, totals[2] * scale)


def solution(mesh):
    placed = (
        P(("groups", "sample"), "space", None, None, None),
        P(),
        P(),
        P(),
        P(("groups", "sample"), None, "space"),
    )
    return jax.shard_map(
        local,
        mesh=mesh,
        in_specs=placed,
        out_specs=(
            P(("groups", "sample"), None, "space"),
            P(("groups", "sample"), "space", None, None, None),
            P(("groups", "space")),
            P(("groups", "space")),
            P(("groups", "space"), None),
        ),
        check_vma=False,
    )
```

profile of v0, /device:TPU:0, one launch (start us, length us, event | category | flops | bytes accessed | tf_op | source)
XLA Modules:
  0.0 502.1 jit_solution(10094833240650439102)
XLA Ops:
  7.2 1.0 fusion.49
  8.1 4.9 collective-permute-start
  13.0 1.3 collective-permute-start.1
  14.3 1.5 slice_bitcast_fusion
  15.9 3.3 collective-permute-done.1
  19.4 0.4 fusion.46
  20.4 0.5 copy-done.33
  24.1 10.2 %reshape.457 = bf16[1,1,16384]{1,0,2:T(2,128)(2,1)} reshape(bf16[64,256]{1,0:T(8,128)(2,1)S(1)} %convolution_convert_fusion) | data formatting | bytes 65536 | tf_op jit(solution)/shard_map/reshape | solution.py:127
  34.3 0.5 broadcast.164
  34.8 123.6 %reduce.5 = bf16[16384]{0:T(1024)(128)(2,1)S(1)} reduce(bf16[16384,1,1]{2,1,0:T(2,128)(2,1)} %bitcast.254, bf16[]{:T(256)} %broadcast.164), dimensions={1,2}, to_apply=%bitcast.187.reduce_sub_computation | reduce | bytes 65538
  158.4 0.6 reshape.465
  159.0 5.8 %all-to-all-start = ((bf16[8,2,1024]{2,1,0:T(2,128)(2,1)}), bf16[8,2,1024]{2,1,0:T(2,128)(2,1)S(1)}, u32[]{:S(2)}, u32[]{:S(2)}) async-start(bf16[8,2,1024]{2,1,0:T(2,128)(2,1)} %reshape.465), calls=%async_computation | async-start | bytes 65536 | tf_op jit(solution)/shard_map/all_to_all | solution.py:128
  164.8 0.6 dynamic-slice
  167.8 3.6 all-to-all-done
  171.5 10.2 %reshape.466 = bf16[16384,1,1]{2,1,0:T(2,128)(2,1)} reshape(bf16[8,2,1024]{2,1,0:T(2,128)(2,1)S(1)} %all-to-all-done) | data formatting | bytes 65536
  181.7 122.9 %bitcast_reduce_fusion = bf16[16384]{0:T(1024)(128)(2,1)S(1)} fusion(bf16[16384,1,1]{2,1,0:T(2,128)(2,1)} %reshape.466), kind=kLoop, calls=%fused_computation.128 | loop fusion | bytes 65536 | tf_op jit(solution)/shard_map/all_to_all | solution.py:128
  305.2 0.8 reduce.6
  306.1 0.6 reshape.467
  306.7 18.2 %all-reduce.4 = f32[8,8]{1,0:T(8,128)S(1)} all-reduce(f32[8,8]{1,0:T(8,128)S(1)} %fusion.39), channel_id=4, replica_groups=mesh['groups'=2,'sample'=2,'space'=8] {'space'}, use_global_device_ids=true, to_apply=%region_4.5.clone | all-reduce | flops 64 | bytes 512
  324.9 0.6 constant_dynamic-slice_fusion
  325.5 3.3 all-to-all-start.1
  328.9 2.5 psum.23
  331.4 0.6 fusion.42
  332.0 0.5 broadcast_multiply_fusion.2
  332.5 2.9 all-to-all-done.1
  336.1 0.3 fusion.10
  336.4 0.6 copy-done.4
  337.3 0.6 copy-done.28
  338.3 0.6 copy-done.22
  339.4 0.6 copy-done.18
  340.0 0.3 fusion.6
  340.4 0.6 copy-done.12
  341.4 0.6 copy-done.6
  342.4 0.3 fusion.3
  342.7 0.3 fusion.2
  343.3 2.4 collective-permute-start.2
  345.7 1.5 collective-permute-start.3
  347.4 0.3 convolution_bitcast_fusion.2
  347.7 1.6 copy.90
  349.3 2.5 collective-permute-done.3
  352.1 0.4 fusion.44
  355.2 116.0 %all-reduce.10.cloned.1.call-done = (f32[442368]{0:T(1024)}, f32[262144]{0:T(1024)}) async-done(((f32[442368]{0:T(1024)}, f32[262144]{0:T(1024)}), (f32[442368]{0:T(1024)}, f32[262144]{0:T(1024)})) %all-reduce.10.cloned.1.call-update) | async-done | bytes 2818064
  471.3 1.6 dynamic-slice.1
  472.9 1.6 dynamic-slice.3
  474.8 0.7 add_convert_fusion
  475.5 16.6 %all-reduce.12.cloned.1.call-done = (f32[55296]{0:T(1024)}, f32[32768]{0:T(1024)}) async-done(((f32[55296]{0:T(1024)}, f32[32768]{0:T(1024)}), (f32[55296]{0:T(1024)}, f32[32768]{0:T(1024)})) %all-reduce.12.cloned.1.call-update) | async-done | bytes 352272 | tf_op jit(solution)/shard_map/psum | solution.py:169
  492.1 1.6 broadcast_multiply_fusion
  493.7 1.6 broadcast_multiply_fusion.1
  (143 shorter events, 11.7 us)
Async XLA Ops:
  7.2 16.8 %copy-start = (bf16[8,128,256]{2,1,0:T(8,128)(2,1)S(1)}, bf16[8,128,256]{2,1,0:T(8,128)(2,1)}, u32[]{:S(2)}) copy-start(bf16[8,128,256]{2,1,0:T(8,128)(2,1)} %param.7) | copy-start | bytes 1572868
  7.2 12.0 %copy-start.1 = (bf16[1,2,16,16,128]{4,3,2,1,0:T(8,128)(2,1)S(1)}, bf16[1,2,16,16,128]{4,3,2,1,0:T(8,128)(2,1)}, u32[]{:S(2)}) copy-start(bf16[1,2,16,16,128]{4,3,2,1,0:T(8,128)(2,1)} %param.5) | copy-start | bytes 393220
  8.1 7.7 %collective-permute-start = (bf16[1,1,16,16,128]{4,3,2,1,0:T(8,128)(2,1)S(1)}, bf16[1,1,16,16,128]{4,3,2,1,0:T(8,128)(2,1)S(1)}, u32[]{:S(2)}, u32[]{:S(2)}) collective-permute-start(bf16[1,1,16,16,128]{4,3,2,1,0:T(8,128)(2,1)S(1)} %get-tuple-element.82), channel_id=1, source_target_pairs={{0,1},{1,2},{2,3},{3,4},{4,5},{5,6},{6,7},{8,9},{9,10},{10,11},{11... | collective-permute-start | bytes 196616 | tf_op jit(solution)/shard_map/ppermute | solution.py:14
  13.0 6.2 %collective-permute-start.1 = (bf16[1,1,16,16,128]{4,3,2,1,0:T(8,128)(2,1)S(1)}, bf16[1,1,16,16,128]{4,3,2,1,0:T(8,128)(2,1)S(1)}, u32[]{:S(2)}, u32[]{:S(2)}) collective-permute-start(bf16[1,1,16,16,128]{4,3,2,1,0:T(8,128)(2,1)S(1)} %get-tuple-element.83), channel_id=1, source_target_pairs={{1,0},{2,1},{3,2},{4,3},{5,4},{6,5},{7,6},{9,8},{10,9},{11,10},{12... | collective-permute-start | bytes 196616 | tf_op jit(solution)/shard_map/ppermute | solution.py:15
  19.7 0.6 copy-start.17
  19.8 0.7 copy-start.19
  19.8 1.7 copy-start.21
  19.8 1.7 copy-start.23
  19.8 1.7 copy-start.25
  19.8 1.7 copy-start.27
  19.8 1.7 copy-start.29
  19.8 1.7 copy-start.31
  19.8 2.7 copy-start.5
  19.8 2.7 copy-start.7
  19.9 2.7 copy-start.9
  19.9 2.7 copy-start.11
  19.9 2.7 copy-start.13
  19.9 2.7 copy-start.15
  20.0 0.9 copy-start.33
  20.0 1.2 copy-start.35
  20.4 1.5 copy-start.3
  34.8 130.0 %copy-start.39 = (u32[32]{0:T(128)S(1)}, u32[32]{0:T(128)}, u32[]{:S(2)}) copy-start(u32[32]{0:T(128)} %constant.22) | copy-start | bytes 388
  159.0 12.4 %all-to-all-start = ((bf16[8,2,1024]{2,1,0:T(2,128)(2,1)}), bf16[8,2,1024]{2,1,0:T(2,128)(2,1)S(1)}, u32[]{:S(2)}, u32[]{:S(2)}) async-start(bf16[8,2,1024]{2,1,0:T(2,128)(2,1)} %reshape.465), calls=%async_computation | async-start | bytes 65536 | tf_op jit(solution)/shard_map/all_to_all | solution.py:128
  181.7 123.0 %copy-start.37 = (bf16[1,8,2048]{2,1,0:T(8,128)(2,1)S(1)}, bf16[1,8,2048]{2,1,0:T(8,128)(2,1)}, u32[]{:S(2)}) copy-start(bf16[1,8,2048]{2,1,0:T(8,128)(2,1)} %param.9) | copy-start | bytes 98308
  181.7 123.0 %copy-start.38 = (bf16[8,8]{1,0:T(8,128)(2,1)S(1)}, bf16[8,8]{1,0:T(8,128)(2,1)}, u32[]{:S(2)}) copy-start(bf16[8,8]{1,0:T(8,128)(2,1)} %param.8) | copy-start | bytes 388
  304.6 31.5 %copy-start.34 = (bf16[1,2,16,16,128]{4,3,2,1,0:T(8,128)(2,1)S(1)}, bf16[1,2,16,16,128]{4,3,2,1,0:T(8,128)(2,1)}, u32[]{:S(2)}) copy-start(bf16[1,2,16,16,128]{4,3,2,1,0:T(8,128)(2,1)} %copy-done.33) | copy-start | bytes 393220
  304.6 31.5 %copy-start.36 = (bf16[1,2,16,16,128]{4,3,2,1,0:T(8,128)(2,1)S(1)}, bf16[1,2,16,16,128]{4,3,2,1,0:T(8,128)(2,1)}, u32[]{:S(2)}) copy-start(bf16[1,2,16,16,128]{4,3,2,1,0:T(8,128)(2,1)} %copy-done.35) | copy-start | bytes 393220
  325.5 10.0 %all-to-all-start.1 = ((bf16[8,2,1024]{2,1,0:T(2,128)(2,1)}), bf16[8,2,1024]{2,1,0:T(2,128)(2,1)S(1)}, u32[]{:S(2)}, u32[]{:S(2)}) async-start(bf16[8,2,1024]{2,1,0:T(2,128)(2,1)} %reshape.467), calls=%async_computation.1 | async-start | bytes 65536 | tf_op jit(solution)/shard_map/all_to_all | solution.py:142
  328.8 142.4 %all-reduce.10.cloned.1.call-start = ((), (), s32[]{:S(2)}) async-start(), calls=%async_computation.2 | async-start | bytes 5636096
  336.0 1.0 copy-start.4
  337.0 0.9 copy-start.28
  337.0 1.0 copy-start.30
  337.0 1.0 copy-start.32
  338.0 0.9 copy-start.22
  338.0 1.0 copy-start.24
  338.0 1.0 copy-start.26
  339.1 0.9 copy-start.18
  339.1 1.0 copy-start.20
  340.0 0.9 copy-start.12
  340.0 1.0 copy-start.14
  340.0 1.0 copy-start.16
  341.1 0.9 copy-start.6
  341.1 1.0 copy-start.8
  341.1 1.0 copy-start.10
  343.0 6.2 %copy-start.2 = (f32[3456,128]{1,0:T(8,128)}, f32[3456,128]{1,0:T(8,128)S(1)}, u32[]{:S(2)}) copy-start(f32[3456,128]{1,0:T(8,128)S(1)} %fusion.2) | copy-start | bytes 5308420
  343.3 6.0 %collective-permute-start.2 = (bf16[1,1,16,16,128]{4,3,2,1,0:T(8,128)(2,1)S(1)}, bf16[1,1,16,16,128]{4,3,2,1,0:T(8,128)(2,1)S(1)}, u32[]{:S(2)}, u32[]{:S(2)}) collective-permute-start(bf16[1,1,16,16,128]{4,3,2,1,0:T(8,128)(2,1)S(1)} %get-tuple-element.77), channel_id=1, source_target_pairs={{0,1},{1,2},{2,3},{3,4},{4,5},{5,6},{6,7},{8,9},{9,10},{10,11},{11... | collective-permute-start | bytes 196616 | tf_op jit(solution)/shard_map/ppermute | solution.py:14
  345.7 6.2 %collective-permute-start.3 = (bf16[1,1,16,16,128]{4,3,2,1,0:T(8,128)(2,1)S(1)}, bf16[1,1,16,16,128]{4,3,2,1,0:T(8,128)(2,1)S(1)}, u32[]{:S(2)}, u32[]{:S(2)}) collective-permute-start(bf16[1,1,16,16,128]{4,3,2,1,0:T(8,128)(2,1)S(1)} %get-tuple-element.78), channel_id=1, source_target_pairs={{1,0},{2,1},{3,2},{4,3},{5,4},{6,5},{7,6},{9,8},{10,9},{11,10},{12... | collective-permute-start | bytes 196616 | tf_op jit(solution)/shard_map/ppermute | solution.py:15
  349.3 142.8 %all-reduce.12.cloned.1.call-start = ((), (), s32[]{:S(2)}) async-start(), calls=%async_computation.3 | async-start | bytes 704512 | tf_op jit(solution)/shard_map/psum | solution.py:169
Sparse Core Ops, SparseCore 0:
  349.4 121.8 all-reduce.9
  474.6 17.4 all-reduce.11
where the time goes:
time: 503 us; the launch traced here: 502 us
  local copies, waits for them, and re-layouts  161 us (32%)
  waiting for transfers between devices  145 us (29%)
  other arithmetic  131 us (26%)
  blocking collectives  20.7 us (4%)
  starting transfers between devices  19.2 us (4%)
  between operations  16.2 us (3%)
  matrix products  8.79 us (2%)
    unnamed x2, other arithmetic  124 us
    all_to_all x2, local copies, waits for them, and re-layouts, local(): lax.all_to_all(coarse, 'space', split_axis=2, concat_axis=1, tiled=True)  123 us
    unnamed x3, waiting for transfers between devices  116 us
    unnamed x90, local copies, waits for them, and re-layouts  22.8 us
    unnamed x1, blocking collectives  18.2 us
    psum x1, waiting for transfers between devices, local(): totals = lax.psum((shares[0], shares[1], shares[2]), 'sample')  16.6 us
    reshape x1, local copies, waits for them, and re-layouts, local(): coarse = coarse.reshape(batch, rows_here // 2, -1)  10.2 us
  transfers between devices with their start and end apart: 8, of which 6 were waited for; matrix products, arithmetic and copies ran while one was open for 2% of the time, Pallas kernels for 0%

commit v1 on v0

--- a/solution.py
+++ b/solution.py
@@ -125,7 +125,10 @@
     down_matrix = w_down.reshape(8 * channels, coarse_ch)
     coarse = jnp.dot(folded, down_matrix, preferred_element_type=jnp.float32).astype(jnp.bfloat16)
     coarse = coarse.reshape(batch, rows_here // 2, -1)
-    columns = lax.all_to_all(coarse, "space", split_axis=2, concat_axis=1, tiled=True)
+    columns = jnp.concatenate(
+        lax.all_to_all(jnp.stack(jnp.split(coarse, lax.axis_size("space"), axis=2)), "space", 0, 0),
+        axis=1,
+    )
     mixed = jnp.stack([jnp.dot(mixing, columns[0], preferred_element_type=jnp.float32)])
     bottleneck = (columns.astype(jnp.float32) + jax.nn.silu(mixed)).astype(jnp.bfloat16)
     cot = cotangent.astype(jnp.float32)

time: 503 us -> 237 us (0.47)
  local copies, waits for them, and re-layouts: 161 us -> 18 us
  other arithmetic: 131 us -> 8.32 us
    unnamed x2 -> x1, other arithmetic: 124 us -> 0.83 us
    all_to_all x2 -> x0, local copies, waits for them, and re-layouts: 123 us -> none  [local(): lax.all_to_all(coarse, 'space', split_axis=2, concat_axis=1, tiled=True)]
    unnamed x90 -> x96, local copies, waits for them, and re-layouts: 22.8 us -> 12.2 us
    reshape x1, local copies, waits for them, and re-layouts: 10.2 us -> 0.02 us  [local(): coarse = coarse.reshape(batch, rows_here // 2, -1)]
  transfers between devices with their start and end apart: 8 -> 8, of which waited for: 6 -> 6; matrix products, arithmetic and copies ran while one was open for 2% -> 4% of each run, Pallas kernels for 0% -> 0%
where the time goes in v1:
time: 237 us; the launch traced here: 236 us
  waiting for transfers between devices  145 us (61%)
  blocking collectives  20.7 us (9%)
  starting transfers between devices  19.2 us (8%)
  local copies, waits for them, and re-layouts  18 us (8%)
  between operations  16.3 us (7%)
  matrix products  8.8 us (4%)
  other arithmetic  8.32 us (4%)
    unnamed x3, waiting for transfers between devices  116 us
    unnamed x1, blocking collectives  18.3 us
    psum x1, waiting for transfers between devices, local(): totals = lax.psum((shares[0], shares[1], shares[2]), 'sample')  16.6 us
    unnamed x96, local copies, waits for them, and re-layouts  12.2 us
    ppermute x2, starting transfers between devices, with_halo(): before = lax.ppermute(last, axis, up)  7.26 us
    ppermute x2, waiting for transfers between devices, with_halo(): after = lax.ppermute(initial, axis, down)  5.93 us
    all_to_all x1, starting transfers between devices, local(): lax.all_to_all(jnp.stack(jnp.split(coarse, lax.axis_size('space'), axis=2...  5.75 us
  transfers between devices with their start and end apart: 8, of which 6 were waited for; matrix products, arithmetic and copies ran while one was open for 4% of the time, Pallas kernels for 0%

profile of v1, /device:TPU:0, one launch (start us, length us, event | category | flops | bytes accessed | tf_op | source)
XLA Modules:
  0.0 236.0 jit_solution(16317323931765933840)
XLA Ops:
  7.2 1.0 fusion.53
  8.1 4.9 %collective-permute-start = (bf16[1,1,16,16,128]{4,3,2,1,0:T(8,128)(2,1)S(1)}, bf16[1,1,16,16,128]{4,3,2,1,0:T(8,128)(2,1)S(1)}, u32[]{:S(2)}, u32[]{:S(2)}) collective-permute-start(bf16[1,1,16,16,128]{4,3,2,1,0:T(8,128)(2,1)S(1)} %get-tuple-element.82), channel_id=1, source_target_pairs={{0,1},{1,2},{2,3},{3,4},{4,5},{5,6},{6,7},{8,9},{9,10},{10,11},{11... | collective-permute-start | bytes 196616 | tf_op jit(solution)/shard_map/ppermute | solution.py:14
  13.0 1.3 collective-permute-start.1
  14.3 1.5 slice_bitcast_fusion.8
  15.9 3.3 %collective-permute-done.1 = bf16[1,1,16,16,128]{4,3,2,1,0:T(8,128)(2,1)S(1)} collective-permute-done((bf16[1,1,16,16,128]{4,3,2,1,0:T(8,128)(2,1)S(1)}, bf16[1,1,16,16,128]{4,3,2,1,0:T(8,128)(2,1)S(1)}, u32[]{:S(2)}, u32[]{:S(2)}) %collective-permute-start.1) | collective-permute-done | bytes 65568 | tf_op jit(solution)/shard_map/ppermute | solution.py:15
  19.4 0.4 fusion.50
  20.5 0.5 copy-done.33
  24.4 0.5 broadcast.163
  24.9 0.8 reduce.3
  25.7 0.6 reshape.463
  26.4 5.8 %all-to-all-start = ((bf16[8,2,1024]{2,1,0:T(2,128)(2,1)}), bf16[8,2,1024]{2,1,0:T(2,128)(2,1)S(1)}, u32[]{:S(2)}, u32[]{:S(2)}) async-start(bf16[8,2,1024]{2,1,0:T(2,128)(2,1)} %reshape.463), calls=%async_computation | async-start | bytes 65536 | tf_op jit(solution)/shard_map/all_to_all | solution.py:129
  32.1 0.6 dynamic-slice
  35.2 3.6 %all-to-all-done = bf16[8,2,1024]{2,1,0:T(2,128)(2,1)S(1)} async-done(((bf16[8,2,1024]{2,1,0:T(2,128)(2,1)}), bf16[8,2,1024]{2,1,0:T(2,128)(2,1)S(1)}, u32[]{:S(2)}, u32[]{:S(2)}) %all-to-all-start) | async-done | bytes 32800 | tf_op jit(solution)/shard_map/all_to_all | solution.py:129
  39.4 0.8 reduce.4
  40.2 0.6 reshape.465
  40.9 18.3 %all-reduce.4 = f32[8,8]{1,0:T(8,128)S(1)} all-reduce(f32[8,8]{1,0:T(8,128)S(1)} %fusion.39), channel_id=4, replica_groups=mesh['groups'=2,'sample'=2,'space'=8] {'space'}, use_global_device_ids=true, to_apply=%region_4.5.clone | all-reduce | flops 64 | bytes 512
  59.1 0.6 constant_dynamic-slice_fusion
  59.8 3.3 %all-to-all-start.1 = ((bf16[8,2,1024]{2,1,0:T(2,128)(2,1)}), bf16[8,2,1024]{2,1,0:T(2,128)(2,1)S(1)}, u32[]{:S(2)}, u32[]{:S(2)}) async-start(bf16[8,2,1024]{2,1,0:T(2,128)(2,1)} %reshape.465), calls=%async_computation.1 | async-start | bytes 65536 | tf_op jit(solution)/shard_map/all_to_all | solution.py:145
  63.2 2.5 %psum.23 = f32[1,8]{1,0:T(1,128)S(1)} all-reduce(f32[1,8]{1,0:T(1,128)S(1)} %constant_dynamic-slice_fusion), channel_id=1, replica_groups=mesh['groups'=2,'sample'=2,'space'=8] {'sample'}, use_global_device_ids=true, to_apply=%region_5.6 | all-reduce | flops 8 | bytes 64 | tf_op jit(solution)/shard_map/psum | solution.py:172
  65.6 0.7 fusion.44
  66.3 0.5 broadcast_multiply_fusion.2
  66.8 2.9 %all-to-all-done.1 = bf16[8,2,1024]{2,1,0:T(2,128)(2,1)S(1)} async-done(((bf16[8,2,1024]{2,1,0:T(2,128)(2,1)}), bf16[8,2,1024]{2,1,0:T(2,128)(2,1)S(1)}, u32[]{:S(2)}, u32[]{:S(2)}) %all-to-all-start.1) | async-done | bytes 32800 | tf_op jit(solution)/shard_map/all_to_all | solution.py:145
  70.4 0.3 fusion.10
  70.7 0.6 copy-done.4
  71.6 0.6 copy-done.28
  72.3 0.3 fusion.8
  72.6 0.6 copy-done.22
  73.6 0.6 copy-done.18
  74.3 0.3 fusion.6
  74.6 0.6 copy-done.12
  75.3 0.3 fusion.5
  75.6 0.6 copy-done.6
  76.4 0.3 fusion.4
  76.7 0.3 fusion.3
  77.0 0.3 fusion.2
  77.6 2.4 %collective-permute-start.2 = (bf16[1,1,16,16,128]{4,3,2,1,0:T(8,128)(2,1)S(1)}, bf16[1,1,16,16,128]{4,3,2,1,0:T(8,128)(2,1)S(1)}, u32[]{:S(2)}, u32[]{:S(2)}) collective-permute-start(bf16[1,1,16,16,128]{4,3,2,1,0:T(8,128)(2,1)S(1)} %get-tuple-element.77), channel_id=1, source_target_pairs={{0,1},{1,2},{2,3},{3,4},{4,5},{5,6},{6,7},{8,9},{9,10},{10,11},{11... | collective-permute-start | bytes 196616 | tf_op jit(solution)/shard_map/ppermute | solution.py:14
  80.0 1.3 collective-permute-start.3
  81.4 0.3 convolution_bitcast_fusion.2
  81.8 1.5 copy.89
  83.6 2.6 %collective-permute-done.3 = bf16[1,1,16,16,128]{4,3,2,1,0:T(8,128)(2,1)S(1)} collective-permute-done((bf16[1,1,16,16,128]{4,3,2,1,0:T(8,128)(2,1)S(1)}, bf16[1,1,16,16,128]{4,3,2,1,0:T(8,128)(2,1)S(1)}, u32[]{:S(2)}, u32[]{:S(2)}) %collective-permute-start.3) | collective-permute-done | bytes 65568 | tf_op jit(solution)/shard_map/ppermute | solution.py:15
  86.3 0.4 fusion.48
  89.5 115.7 %all-reduce.10.cloned.1.call-done = (f32[442368]{0:T(1024)}, f32[262144]{0:T(1024)}) async-done(((f32[442368]{0:T(1024)}, f32[262144]{0:T(1024)}), (f32[442368]{0:T(1024)}, f32[262144]{0:T(1024)})) %all-reduce.10.cloned.1.call-update) | async-done | bytes 2818064
  205.2 1.6 dynamic-slice.1
  206.8 1.6 dynamic-slice.3
  208.7 0.7 add_convert_fusion
  209.4 16.6 %all-reduce.12.cloned.1.call-done = (f32[55296]{0:T(1024)}, f32[32768]{0:T(1024)}) async-done(((f32[55296]{0:T(1024)}, f32[32768]{0:T(1024)}), (f32[55296]{0:T(1024)}, f32[32768]{0:T(1024)})) %all-reduce.12.cloned.1.call-update) | async-done | bytes 352272 | tf_op jit(solution)/shard_map/psum | solution.py:172
  226.0 1.6 broadcast_multiply_fusion
  227.6 1.6 broadcast_multiply_fusion.1
  (149 shorter events, 11.2 us)
Async XLA Ops:
  7.2 16.8 %copy-start = (bf16[8,128,256]{2,1,0:T(8,128)(2,1)S(1)}, bf16[8,128,256]{2,1,0:T(8,128)(2,1)}, u32[]{:S(2)}) copy-start(bf16[8,128,256]{2,1,0:T(8,128)(2,1)} %param.7) | copy-start | bytes 1572868
  7.2 12.0 %copy-start.1 = (bf16[1,2,16,16,128]{4,3,2,1,0:T(8,128)(2,1)S(1)}, bf16[1,2,16,16,128]{4,3,2,1,0:T(8,128)(2,1)}, u32[]{:S(2)}) copy-start(bf16[1,2,16,16,128]{4,3,2,1,0:T(8,128)(2,1)} %param.5) | copy-start | bytes 393220
  8.1 7.7 %collective-permute-start = (bf16[1,1,16,16,128]{4,3,2,1,0:T(8,128)(2,1)S(1)}, bf16[1,1,16,16,128]{4,3,2,1,0:T(8,128)(2,1)S(1)}, u32[]{:S(2)}, u32[]{:S(2)}) collective-permute-start(bf16[1,1,16,16,128]{4,3,2,1,0:T(8,128)(2,1)S(1)} %get-tuple-element.82), channel_id=1, source_target_pairs={{0,1},{1,2},{2,3},{3,4},{4,5},{5,6},{6,7},{8,9},{9,10},{10,11},{11... | collective-permute-start | bytes 196616 | tf_op jit(solution)/shard_map/ppermute | solution.py:14
  13.0 6.2 %collective-permute-start.1 = (bf16[1,1,16,16,128]{4,3,2,1,0:T(8,128)(2,1)S(1)}, bf16[1,1,16,16,128]{4,3,2,1,0:T(8,128)(2,1)S(1)}, u32[]{:S(2)}, u32[]{:S(2)}) collective-permute-start(bf16[1,1,16,16,128]{4,3,2,1,0:T(8,128)(2,1)S(1)} %get-tuple-element.83), channel_id=1, source_target_pairs={{1,0},{2,1},{3,2},{4,3},{5,4},{6,5},{7,6},{9,8},{10,9},{11,10},{12... | collective-permute-start | bytes 196616 | tf_op jit(solution)/shard_map/ppermute | solution.py:15
  19.7 0.7 copy-start.17
  19.8 0.7 copy-start.19
  19.8 1.7 copy-start.21
  19.8 1.7 copy-start.23
  19.8 1.7 copy-start.25
  19.8 1.7 copy-start.27
  19.8 1.7 copy-start.29
  19.8 1.7 copy-start.31
  19.8 2.7 %copy-start.5 = (bf16[1,2,16,16,128]{4,3,2,1,0:T(8,128)(2,1)}, bf16[1,2,16,16,128]{4,3,2,1,0:T(8,128)(2,1)S(1)}, u32[]{:S(2)}) copy-start(bf16[1,2,16,16,128]{4,3,2,1,0:T(8,128)(2,1)S(1)} %get-tuple-element.55) | copy-start | bytes 393220
  19.8 2.7 %copy-start.7 = (bf16[1,2,16,16,128]{4,3,2,1,0:T(8,128)(2,1)}, bf16[1,2,16,16,128]{4,3,2,1,0:T(8,128)(2,1)S(1)}, u32[]{:S(2)}) copy-start(bf16[1,2,16,16,128]{4,3,2,1,0:T(8,128)(2,1)S(1)} %get-tuple-element.56) | copy-start | bytes 393220
  19.9 2.7 %copy-start.9 = (bf16[1,2,16,16,128]{4,3,2,1,0:T(8,128)(2,1)}, bf16[1,2,16,16,128]{4,3,2,1,0:T(8,128)(2,1)S(1)}, u32[]{:S(2)}) copy-start(bf16[1,2,16,16,128]{4,3,2,1,0:T(8,128)(2,1)S(1)} %get-tuple-element.57) | copy-start | bytes 393220
  19.9 2.7 %copy-start.11 = (bf16[1,2,16,16,128]{4,3,2,1,0:T(8,128)(2,1)}, bf16[1,2,16,16,128]{4,3,2,1,0:T(8,128)(2,1)S(1)}, u32[]{:S(2)}) copy-start(bf16[1,2,16,16,128]{4,3,2,1,0:T(8,128)(2,1)S(1)} %get-tuple-element.58) | copy-start | bytes 393220
  19.9 2.7 %copy-start.13 = (bf16[1,2,16,16,128]{4,3,2,1,0:T(8,128)(2,1)}, bf16[1,2,16,16,128]{4,3,2,1,0:T(8,128)(2,1)S(1)}, u32[]{:S(2)}) copy-start(bf16[1,2,16,16,128]{4,3,2,1,0:T(8,128)(2,1)S(1)} %get-tuple-element.59) | copy-start | bytes 393220
  19.9 2.7 %copy-start.15 = (bf16[1,2,16,16,128]{4,3,2,1,0:T(8,128)(2,1)}, bf16[1,2,16,16,128]{4,3,2,1,0:T(8,128)(2,1)S(1)}, u32[]{:S(2)}) copy-start(bf16[1,2,16,16,128]{4,3,2,1,0:T(8,128)(2,1)S(1)} %get-tuple-element.60) | copy-start | bytes 393220
  20.0 0.9 copy-start.33
  20.0 1.2 copy-start.35
  20.5 1.5 copy-start.3
  23.5 8.6 %copy-start.39 = (u32[32]{0:T(128)S(1)}, u32[32]{0:T(128)}, u32[]{:S(2)}) copy-start(u32[32]{0:T(128)} %constant.22) | copy-start | bytes 388
  23.9 14.9 %copy-start.37 = (bf16[1,8,2048]{2,1,0:T(8,128)(2,1)S(1)}, bf16[1,8,2048]{2,1,0:T(8,128)(2,1)}, u32[]{:S(2)}) copy-start(bf16[1,8,2048]{2,1,0:T(8,128)(2,1)} %param.9) | copy-start | bytes 98308
  23.9 14.9 %copy-start.38 = (bf16[8,8]{1,0:T(8,128)(2,1)S(1)}, bf16[8,8]{1,0:T(8,128)(2,1)}, u32[]{:S(2)}) copy-start(bf16[8,8]{1,0:T(8,128)(2,1)} %param.8) | copy-start | bytes 388
  26.4 12.4 %all-to-all-start = ((bf16[8,2,1024]{2,1,0:T(2,128)(2,1)}), bf16[8,2,1024]{2,1,0:T(2,128)(2,1)S(1)}, u32[]{:S(2)}, u32[]{:S(2)}) async-start(bf16[8,2,1024]{2,1,0:T(2,128)(2,1)} %reshape.463), calls=%async_computation | async-start | bytes 65536 | tf_op jit(solution)/shard_map/all_to_all | solution.py:129
  35.2 35.2 %copy-start.34 = (bf16[1,2,16,16,128]{4,3,2,1,0:T(8,128)(2,1)S(1)}, bf16[1,2,16,16,128]{4,3,2,1,0:T(8,128)(2,1)}, u32[]{:S(2)}) copy-start(bf16[1,2,16,16,128]{4,3,2,1,0:T(8,128)(2,1)} %copy-done.33) | copy-start | bytes 393220
  35.2 35.2 %copy-start.36 = (bf16[1,2,16,16,128]{4,3,2,1,0:T(8,128)(2,1)S(1)}, bf16[1,2,16,16,128]{4,3,2,1,0:T(8,128)(2,1)}, u32[]{:S(2)}) copy-start(bf16[1,2,16,16,128]{4,3,2,1,0:T(8,128)(2,1)} %copy-done.35) | copy-start | bytes 393220
  59.8 10.0 %all-to-all-start.1 = ((bf16[8,2,1024]{2,1,0:T(2,128)(2,1)}), bf16[8,2,1024]{2,1,0:T(2,128)(2,1)S(1)}, u32[]{:S(2)}, u32[]{:S(2)}) async-start(bf16[8,2,1024]{2,1,0:T(2,128)(2,1)} %reshape.465), calls=%async_computation.1 | async-start | bytes 65536 | tf_op jit(solution)/shard_map/all_to_all | solution.py:145
  63.1 142.1 %all-reduce.10.cloned.1.call-start = ((), (), s32[]{:S(2)}) async-start(), calls=%async_computation.2 | async-start | bytes 5636096
  70.3 1.0 copy-start.4
  71.3 0.9 copy-start.28
  71.3 1.0 copy-start.30
  71.3 1.0 copy-start.32
  72.3 0.9 copy-start.22
  72.3 1.0 copy-start.24
  72.3 1.0 copy-start.26
  73.3 0.9 copy-start.18
  73.3 1.0 copy-start.20
  74.3 0.9 copy-start.12
  74.3 1.0 copy-start.14
  74.3 1.0 copy-start.16
  75.3 0.9 copy-start.6
  75.3 1.0 copy-start.8
  75.3 1.0 copy-start.10
  77.3 6.0 %copy-start.2 = (f32[3456,128]{1,0:T(8,128)}, f32[3456,128]{1,0:T(8,128)S(1)}, u32[]{:S(2)}) copy-start(f32[3456,128]{1,0:T(8,128)S(1)} %fusion.2) | copy-start | bytes 5308420
  77.6 5.9 %collective-permute-start.2 = (bf16[1,1,16,16,128]{4,3,2,1,0:T(8,128)(2,1)S(1)}, bf16[1,1,16,16,128]{4,3,2,1,0:T(8,128)(2,1)S(1)}, u32[]{:S(2)}, u32[]{:S(2)}) collective-permute-start(bf16[1,1,16,16,128]{4,3,2,1,0:T(8,128)(2,1)S(1)} %get-tuple-element.77), channel_id=1, source_target_pairs={{0,1},{1,2},{2,3},{3,4},{4,5},{5,6},{6,7},{8,9},{9,10},{10,11},{11... | collective-permute-start | bytes 196616 | tf_op jit(solution)/shard_map/ppermute | solution.py:14
  80.0 6.2 %collective-permute-start.3 = (bf16[1,1,16,16,128]{4,3,2,1,0:T(8,128)(2,1)S(1)}, bf16[1,1,16,16,128]{4,3,2,1,0:T(8,128)(2,1)S(1)}, u32[]{:S(2)}, u32[]{:S(2)}) collective-permute-start(bf16[1,1,16,16,128]{4,3,2,1,0:T(8,128)(2,1)S(1)} %get-tuple-element.78), channel_id=1, source_target_pairs={{1,0},{2,1},{3,2},{4,3},{5,4},{6,5},{7,6},{9,8},{10,9},{11,10},{12... | collective-permute-start | bytes 196616 | tf_op jit(solution)/shard_map/ppermute | solution.py:15
  83.3 142.7 %all-reduce.12.cloned.1.call-start = ((), (), s32[]{:S(2)}) async-start(), calls=%async_computation.3 | async-start | bytes 704512 | tf_op jit(solution)/shard_map/psum | solution.py:172
Sparse Core Ops, SparseCore 0:
  83.4 121.6 all-reduce.9
  208.5 17.4 all-reduce.11
